TPU v7x, 256 devices: a whole 4x4x8 slice. The times are simulated.
256 devices in a mesh: ctx: 32 (over z_hi, x, core), head: 8 (over z_lo, y).
Axes of the slice: x: 4, y: 4, z: 8 (z_hi: 4, z_lo: 2; z = z_hi * 2 + z_lo), core: 2. Of those that a mesh axis runs over, the one named last changes fastest.
Arguments:
- activations: bfloat16 [4096, 8192], P('ctx', 'head'), may hold values from -6 to 6
- query_base: bfloat16 [4096, 8192], P('ctx', 'head'), may hold values from -150 to 150
- key_rows: bfloat16 [4096, 1024], P('ctx', 'head'), may hold values from -4 to 4
- values: bfloat16 [4096, 1024], P('ctx', 'head'), may hold values from -6 to 6
- out_cotangent: bfloat16 [4096, 8192], P('ctx', 'head'), may hold values from -0.3984375 to 0.3984375
- adapter_a: bfloat16 [8192, 16], P('head'), may hold values from -0.0625 to 0.0625
- adapter_b: bfloat16 [16, 8192], P(None, 'head'), may hold values from -1.5 to 1.5
- tangent_a: bfloat16 [8192, 16], P('head'), may hold values from -0.0625 to 0.0625
- tangent_b: bfloat16 [16, 8192], P(None, 'head'), may hold values from -1.5 to 1.5
- segment_ids: int32 [4096], P('ctx'), may hold values from 0 to 7, as said below
- doc_starts: int32 [8], replicated, may hold values from 0 to 4095, as said below
Outputs:
- hvp_a: float32 [8192, 16], P('head')
- hvp_b: float32 [16, 8192], P(None, 'head')
Inputs may be any that keep to these rules, and one draw needn't show every extreme that they name: `segment_ids`: segment numbers never fall along the tokens, and every number from 0 to 7 occurs. doc_starts[s] is the first position of segment s; starts rise strictly, doc_starts[0] is 0, every later start is 2560 or more, and the last is 4095.
All inputs are finite; a program needn't handle non-finite values.
Results may differ from a plain program's by a relative error of at most 0.0091.
Values may be sent and summed in bfloat16 or wider, within the bound.
A program may use at most 64 MiB of HBM per device.

v0:
```python
import math

import jax
import jax.numpy as jnp
from jax import lax
from jax.sharding import PartitionSpec as P

QUERY_HEADS = 64
KEY_VALUE_HEADS = 8
HEAD_SIZE = 128
ADAPTER_RANK = 16


masked_value = -1e30


def visible_mask(positions, row_starts, first_key, key_count):
    key_pos = first_key + jnp.arange(key_count, dtype=jnp.int32)
    return (key_pos[None, :] <= positions[:, None]) & (key_pos[None, :] >= row_starts[:, None])


def empty_state(row_count, query_group):
    zero_fill = jnp.zeros((row_count, query_group), jnp.float32)
    return (
        jnp.full((row_count, query_group), masked_value, jnp.float32),
        zero_fill,
        zero_fill,
        zero_fill,
        zero_fill,
        jnp.zeros((4, row_count, query_group, HEAD_SIZE), jnp.float32),
    )


def absorb(current, queries, tangents, cotangents, key_blk, value_blk, visible, score_scale):
    running_max, weight_sum, along_sum, slope_sum, cross_sum, key_sums = current
    scores = (
        jnp.einsum("rgd,kd->rgk", queries, key_blk, preferred_element_type=jnp.float32)
        * score_scale
    )
    slopes = (
        jnp.einsum("rgd,kd->rgk", tangents, key_blk, preferred_element_type=jnp.float32)
        * score_scale
    )
    value_dots = jnp.einsum(
        "rgd,kd->rgk", cotangents, value_blk, preferred_element_type=jnp.float32
    )
    mask_three = visible[:, None, :]
    fresh_max = jnp.maximum(
        running_max, jnp.max(jnp.where(mask_three, scores, masked_value), axis=2)
    )
    factor = jnp.exp(running_max - fresh_max)
    weights = jnp.where(mask_three, jnp.exp(scores - fresh_max[..., None]), 0.0)
    weighted_dots = weights * value_dots
    weighted_slopes = weights * slopes
    weighted_both = weighted_slopes * value_dots
    weight_sum = weight_sum * factor + jnp.sum(weights, axis=2)
    along_sum = along_sum * factor + jnp.sum(weighted_dots, axis=2)
    slope_sum = slope_sum * factor + jnp.sum(weighted_slopes, axis=2)
    cross_sum = cross_sum * factor + jnp.sum(weighted_both, axis=2)
    stacked = jnp.stack([weights, weighted_dots, weighted_slopes, weighted_both]).astype(
        jnp.bfloat16
    )
    key_sums = key_sums * factor[None, :, :, None] + jnp.einsum(
        "trgk,kd->trgd", stacked, key_blk, preferred_element_type=jnp.float32
    )
    return (fresh_max, weight_sum, along_sum, slope_sum, cross_sum, key_sums)


def finish(held, score_scale):
    running_max, weight_sum, along_sum, slope_sum, cross_sum, key_sums = held
    delta = along_sum / weight_sum
    mean_slope = slope_sum / weight_sum
    delta_dot = cross_sum / weight_sum - mean_slope * delta
    factor = score_scale / weight_sum
    grad = (key_sums[1] - delta[..., None] * key_sums[0]) * factor[..., None]
    grad_dot = (
        key_sums[3]
        - delta[..., None] * key_sums[2]
        - mean_slope[..., None] * key_sums[1]
        + (mean_slope * delta - delta_dot)[..., None] * key_sums[0]
    ) * factor[..., None]
    return (grad, grad_dot)


def on_device(
    activations,
    query_base,
    key_rows,
    values,
    out_cotangent,
    adapter_a,
    adapter_b,
    tangent_a,
    tangent_b,
    segment_ids,
    doc_starts,
):
    highest = lax.Precision.HIGHEST
    score_scale = 1.0 / math.sqrt(HEAD_SIZE)
    query_group = QUERY_HEADS // KEY_VALUE_HEADS
    row_count = activations.shape[0]
    half_rows = row_count // 2
    ctx_index = lax.axis_index("ctx")
    home = ctx_index * row_count + jnp.arange(row_count, dtype=jnp.int32)
    x_rows, q_rows, cot_rows, seg_rows = (activations, query_base, out_cotangent, segment_ids)
    doc_count = doc_starts.shape[0]
    row_starts = jnp.sum(
        jnp.where(
            seg_rows[:, None] == jnp.arange(doc_count, dtype=jnp.int32)[None, :],
            doc_starts[None, :],
            0,
        ),
        axis=1,
    )
    both_a = jnp.concatenate([adapter_a, tangent_a], axis=1)
    partial_low = jnp.dot(x_rows, both_a, preferred_element_type=jnp.float32)
    adapted = lax.psum(partial_low, "head")
    low = adapted[:, :ADAPTER_RANK]
    low_tangent = adapted[:, ADAPTER_RANK:]
    b_wide = adapter_b.astype(jnp.float32)
    b_tangent = tangent_b.astype(jnp.float32)
    queries = (q_rows.astype(jnp.float32) + jnp.dot(low, b_wide, precision=highest)).astype(
        jnp.bfloat16
    )
    query_tangent = (
        jnp.dot(low_tangent, b_wide, precision=highest) + jnp.dot(low, b_tangent, precision=highest)
    ).astype(jnp.bfloat16)
    members = []
    key_value_head = 0
    q_three = queries.reshape(row_count, query_group, HEAD_SIZE)
    t_three = query_tangent.reshape(row_count, query_group, HEAD_SIZE)
    g_three = cot_rows.reshape(row_count, query_group, HEAD_SIZE)
    for half_index in range(2):
        rows_here = slice(half_index * half_rows, (half_index + 1) * half_rows)
        members.append(
            (
                key_value_head,
                q_three[rows_here],
                t_three[rows_here],
                g_three[rows_here],
                home[rows_here],
                row_starts[rows_here],
            )
        )
    initial = tuple((empty_state(half_rows, query_group) for member in members))
    key_piece = lax.all_gather(key_rows, "ctx", axis=0, tiled=True)
    value_piece = lax.all_gather(values, "ctx", axis=0, tiled=True)
    key_count = key_piece.shape[0]
    block_len = math.gcd(key_count, 512)

    def one_block(block_step, inner_carried):
        first_key = block_step * block_len
        key_all = lax.dynamic_slice_in_dim(key_piece, block_step * block_len, block_len, 0)
        value_all = lax.dynamic_slice_in_dim(value_piece, block_step * block_len, block_len, 0)
        updated = []
        for slot_index, member in enumerate(members):
            key_value_head, q_half, t_half, g_half, pos_half, start_half = member
            key_blk = key_all
            value_blk = value_all
            visible = visible_mask(pos_half, start_half, first_key, block_len)

            def apply_block(
                held,
                q_half=q_half,
                t_half=t_half,
                g_half=g_half,
                key_blk=key_blk,
                value_blk=value_blk,
                visible=visible,
            ):
                return absorb(
                    held, q_half, t_half, g_half, key_blk, value_blk, visible, score_scale
                )

            current = apply_block(inner_carried[slot_index])
            updated.append(current)
        return tuple(updated)

    finals = lax.fori_loop(0, key_count // block_len, one_block, initial)
    key_value_head = 0
    halves = [
        finish(finals[key_value_head * 2 + half_index], score_scale) for half_index in range(2)
    ]
    grad_heads = jnp.concatenate([halves[0][0], halves[1][0]], axis=0).reshape(
        row_count, query_group * HEAD_SIZE
    )
    grad_dot_heads = jnp.concatenate([halves[0][1], halves[1][1]], axis=0).reshape(
        row_count, query_group * HEAD_SIZE
    )
    z_part = jnp.dot(grad_dot_heads, b_wide.T, precision=highest) + jnp.dot(
        grad_heads, b_tangent.T, precision=highest
    )
    b_part = jnp.dot(low_tangent.T, grad_heads, precision=highest) + jnp.dot(
        low.T, grad_dot_heads, precision=highest
    )
    z_full = lax.psum(z_part, "head")
    a_part = jnp.dot(x_rows.astype(jnp.float32).T, z_full, precision=highest)
    hvp_a, hvp_b = lax.psum((a_part, b_part), "ctx")
    return (hvp_a, hvp_b)


def solution(mesh):
    placed = (
        P("ctx", "head"),
        P("ctx", "head"),
        P("ctx", "head"),
        P("ctx", "head"),
        P("ctx", "head"),
        P("head", None),
        P(None, "head"),
        P("head", None),
        P(None, "head"),
        P("ctx"),
        P(),
    )
    return jax.shard_map(
        on_device,
        mesh=mesh,
        in_specs=placed,
        out_specs=(P("head", None), P(None, "head")),
        check_vma=False,
    )
```

profile of v0, /device:TPU:1, one launch (start us, length us, event | category | flops | bytes accessed | tf_op | source)
XLA Modules:
  0.0 588.0 jit_solution(18232348498028754442)
XLA Ops:
  9.8 29.1 %psum.28 = f32[128,32]{0,1:T(8,128)S(1)} all-reduce(f32[128,32]{0,1:T(8,128)S(1)} %convolution_bitcast_fusion.3), channel_id=1, replica_groups=mesh['ctx'=32,'head'=8] {'head'}, use_global_device_ids=true, to_apply=%region_1.2 | all-reduce | flops 4096 | bytes 32768 | tf_op jit(solution)/shard_map/psum | solution.py:117
  44.0 22.7 %all-gather.3.cloned.1.call-done = bf16[4096,128]{1,0:T(8,128)(2,1)} async-done(((bf16[128,128]{1,0:T(8,128)(2,1)}), bf16[4096,128]{1,0:T(8,128)(2,1)}) %all-gather.3.cloned.1.call-update) | async-done | bytes 1048592 | tf_op jit(solution)/shard_map/all_gather | solution.py:146
  66.8 52.1 %all-gather.5.cloned.1.call-done = bf16[4096,128]{1,0:T(8,128)(2,1)} async-done(((bf16[128,128]{1,0:T(8,128)(2,1)}), bf16[4096,128]{1,0:T(8,128)(2,1)}) %all-gather.5.cloned.1.call-update) | async-done | bytes 1048592 | tf_op jit(solution)/shard_map/all_gather | solution.py:147
  118.8 172.0 %while.36 = (s32[]{:T(128)}, f32[64,8]{0,1:T(8,128)S(1)}, f32[64,8]{0,1:T(8,128)}, f32[64,8]{0,1:T(8,128)}, f32[64,8]{0,1:T(8,128)}, /*index=5*/f32[64,8]{0,1:T(...) while((s32[]{:T(128)}, f32[64,8]{0,1:T(8,128)S(1)}, ...), condition=%wide.region_13.14_spmd.clone, body=%wide.region_2.13_spmd.clone.sunk | while | flops 956509696 | bytes 52124016 | solution.py:179
  122.8 1.9 multiply_reduce_fusion.6
  126.1 2.5 multiply_reduce_fusion.7
  132.8 2.4 fusion.135
  136.8 2.5 fusion.133
  144.3 1.9 multiply_reduce_fusion.6
  147.6 2.5 multiply_reduce_fusion.7
  154.3 2.4 fusion.135
  158.3 2.5 fusion.133
  169.1 2.5 multiply_reduce_fusion.7
  175.8 2.4 fusion.135
  179.8 2.5 fusion.133
  190.6 2.5 multiply_reduce_fusion.7
  197.3 2.4 fusion.135
  201.3 2.5 fusion.133
  212.1 2.5 multiply_reduce_fusion.7
  218.8 2.4 fusion.135
  222.8 2.5 fusion.133
  233.6 2.5 multiply_reduce_fusion.7
  240.3 2.4 fusion.135
  244.3 2.5 fusion.133
  255.1 2.5 multiply_reduce_fusion.7
  261.8 2.4 fusion.135
  265.8 2.5 fusion.133
  276.7 2.5 multiply_reduce_fusion.7
  283.3 2.4 fusion.135
  287.3 2.5 fusion.133
  298.6 14.7 %psum.29 = f32[128,16]{0,1:T(8,128)S(1)} all-reduce(f32[128,16]{0,1:T(8,128)S(1)} %convolution_add_fusion.3), channel_id=1, replica_groups=mesh['ctx'=32,'head'=8] {'head'}, use_global_device_ids=true, to_apply=%region_14.15 | all-reduce | flops 2048 | bytes 16384 | tf_op jit(solution)/shard_map/psum | solution.py:196
  314.1 264.4 %all-reduce.3.cloned.1.call-done = (f32[1024,16]{0,1:T(8,128)}, f32[16,1024]{1,0:T(8,128)}) async-done(((f32[1024,16]{0,1:T(8,128)}, f32[16,1024]{1,0:T(8,128)}), (f32[1024,16]{0,1:T(8,128)}, f32[16,1024]{1,0:T(8,128)})) %all-reduce.3.cloned.1.call-update) | async-done | bytes 131088 | tf_op jit(solution)/shard_map/psum | solution.py:198
  (810 shorter events, 124.4 us)
Async XLA Ops:
  7.2 35.1 %copy-start.15 = (bf16[16,1024]{1,0:T(8,128)(2,1)S(1)}, bf16[16,1024]{1,0:T(8,128)(2,1)}, u32[]{:S(2)}) copy-start(bf16[16,1024]{1,0:T(8,128)(2,1)} %param.19) | copy-start | bytes 98308
  7.2 35.5 %copy-start.35 = (bf16[16,1024]{1,0:T(8,128)(2,1)S(1)}, bf16[16,1024]{1,0:T(8,128)(2,1)}, u32[]{:S(2)}) copy-start(bf16[16,1024]{1,0:T(8,128)(2,1)} %param.21) | copy-start | bytes 98308
  7.2 59.6 %all-gather.3.cloned.1.call-start = ((), (), s32[]{:S(2)}) async-start(), calls=%async_computation | async-start | bytes 1081344 | tf_op jit(solution)/shard_map/all_gather | solution.py:146
  7.9 110.9 %all-gather.5.cloned.1.call-start = ((), (), s32[]{:S(2)}) async-start(), calls=%async_computation.1 | async-start | bytes 1081344 | tf_op jit(solution)/shard_map/all_gather | solution.py:147
  8.7 569.8 %all-reduce.3.cloned.1.call-start = ((), (), s32[]{:S(2)}) async-start(), calls=%async_computation.2 | async-start | bytes 262144 | tf_op jit(solution)/shard_map/psum | solution.py:198
  39.0 4.2 copy-start.17
  118.9 3.9 copy-start.41
  118.9 3.9 copy-start.43
  118.9 5.8 copy-start.37
  140.3 3.9 copy-start.6
  140.4 5.8 copy-start.37
  161.8 3.9 copy-start.6
  161.8 3.9 copy-start.8
  161.8 3.9 copy-start.10
  161.9 3.9 copy-start.39
  161.9 3.9 copy-start.41
  161.9 3.9 copy-start.43
  161.9 5.8 copy-start.37
  183.3 3.9 copy-start.6
  183.4 5.8 copy-start.37
  204.8 3.9 copy-start.6
  204.9 5.8 copy-start.37
  226.3 3.9 copy-start.6
  226.4 3.9 copy-start.8
  226.4 3.9 copy-start.10
  226.4 3.9 copy-start.39
  226.4 3.9 copy-start.41
  226.4 5.8 copy-start.37
  247.9 3.9 copy-start.6
  247.9 5.8 copy-start.37
  269.4 3.9 copy-start.6
  269.4 5.8 copy-start.37
  (275 other events, 618.9 us)
Sparse Core Ops, SparseCore 0:
  10.6 56.1 all-gather.2
  69.3 49.4 all-gather.4
  314.3 264.1 all-reduce.2
where the time goes:
time: 590 us; the launch traced here: 588 us
  waiting for transfers between devices  341 us (58%)
  matrix products  119 us (20%)
  local copies, waits for them, and re-layouts  46.6 us (8%)
  blocking collectives  43.9 us (7%)
  other arithmetic  19.1 us (3%)
  between operations  14.1 us (2%)
    psum x1, waiting for transfers between devices, on_device(): hvp_a, hvp_b = lax.psum((a_part, b_part), 'ctx')  264 us
    all_gather x1, waiting for transfers between devices, on_device(): value_piece = lax.all_gather(values, 'ctx', axis=0, tiled=True)  52.1 us
    dot_general x16, matrix products, absorb(): jnp.einsum('trgk,kd->trgd', stacked, key_blk, preferred_element_type=jnp....  38.7 us
    dot_general x16, matrix products, absorb(): jnp.einsum('rgd,kd->rgk', tangents, key_blk, preferred_element_type=jnp.f...  34.8 us
    psum x1, blocking collectives, on_device(): adapted = lax.psum(partial_low, 'head')  29.1 us
    while x608, local copies, waits for them, and re-layouts  27.5 us
    all_gather x1, waiting for transfers between devices, on_device(): key_piece = lax.all_gather(key_rows, 'ctx', axis=0, tiled=True)  22.7 us
    dot_general x16, matrix products, absorb(): jnp.einsum('rgd,kd->rgk', queries, key_blk, preferred_element_type=jnp.fl...  20.5 us
  transfers between devices with their start and end apart: 3, of which 3 were waited for; matrix products, arithmetic and copies ran while one was open for 1% of the time, Pallas kernels for 0%

commit v1 on v0

v1 whole, which is shorter than its diff:
```python
import functools, math
import jax, jax.numpy as jnp
from jax import lax
from jax.experimental import pallas as pl
from jax.experimental.pallas import tpu as pltpu

HS = 128
NT = (((1,), (1,)), ((), ()))
TN = (((0,), (0,)), ((), ()))
NN = (((1,), (0,)), ((), ()))
f32, bf16 = jnp.float32, jnp.bfloat16


def mm(a, b, dims=NN):
    return lax.dot_general(a, b, dims, preferred_element_type=f32)


def split2(x):
    hi = x.astype(bf16)
    return hi, (x - hi.astype(f32)).astype(bf16)


def split3(x):
    hi = x.astype(bf16)
    r = x - hi.astype(f32)
    mid = r.astype(bf16)
    return hi, mid, (r - mid.astype(f32)).astype(bf16)


def attend_kernel(kb_len, base_fn, docs, seg_s, seg_v, low_ref, qb_ref, cot_ref, b_ref, tb_ref, k_ref, v_ref,
                  z_ref, bp_ref, s_buf, kt, acc, m_ref, q_s, t_s, g_s):
    rows = qb_ref.shape[0]
    heads = qb_ref.shape[1] // HS
    tile = 2
    lanes = tile * rows
    base = base_fn()
    scale = 1.0 / math.sqrt(HS)
    cexp = scale * math.log2(math.e)
    start_first = docs[seg_s[0]]
    start_last = docs[seg_s[rows - 1]]
    lo = start_first // kb_len
    hi = (base + rows - 1) // kb_len + 1
    seg = seg_v[...]
    starts = jnp.zeros((1, rows), jnp.int32)
    for d in range(docs.shape[0]):
        starts = jnp.where(seg == d, docs[d], starts)
    pos = base + lax.broadcasted_iota(jnp.int32, (1, rows), 1)
    starts2 = jnp.concatenate([starts] * tile, axis=1)
    pos2 = jnp.concatenate([pos] * tile, axis=1)

    low = low_ref[0:16, :]
    lowt = low_ref[16:32, :]
    l3 = split3(low)
    lt3 = split3(lowt)
    b = b_ref[...]
    tb = tb_ref[...]
    q_all = mm(jnp.concatenate(l3, 0), jnp.concatenate([b, b, b], 0), TN) + qb_ref[...].astype(f32)
    t_all = mm(jnp.concatenate(lt3 + l3, 0), jnp.concatenate([b, b, b, tb, tb, tb], 0), TN)
    for h in range(heads):
        cols = slice(h * HS, (h + 1) * HS)
        q_s[h] = q_all[:, cols].astype(bf16)
        t_s[h] = t_all[:, cols].astype(bf16)
        g_s[h] = cot_ref[:, cols]

    def build(kb, c):
        off = pl.multiple_of(kb * kb_len, kb_len)
        kt[0:HS, pl.ds(off, kb_len)] = k_ref[pl.ds(off, kb_len), :].T
        kt[HS:HS + 16, pl.ds(off, kb_len)] = jnp.ones((16, kb_len), bf16)
        return c

    lax.fori_loop(lo, hi, build, 0)
    llt = jnp.concatenate([lt3[0], lt3[0], lt3[1], l3[0], l3[0], l3[1]], axis=1)
    z_ref[...] = jnp.zeros_like(z_ref)

    def one_tile(ti, carry):
        q2 = q_s[pl.ds(ti * tile, tile)].reshape(lanes, HS)
        t2 = t_s[pl.ds(ti * tile, tile)].reshape(lanes, HS)
        g2 = g_s[pl.ds(ti * tile, tile)].reshape(lanes, HS)
        m_ref[...] = jnp.full(m_ref.shape, -1e30, f32)

        def pass1(kb, c):
            off = pl.multiple_of(kb * kb_len, kb_len)
            need = (off < start_last) | (off + kb_len - 1 > base)

            @pl.when(need)
            def _():
                s = mm(k_ref[pl.ds(off, kb_len), :], q2, NT)
                kp = off + lax.broadcasted_iota(jnp.int32, (kb_len, lanes), 0)
                s = jnp.where((kp >= starts2) & (kp <= pos2), s, -1e30)
                s_buf[pl.ds(off, kb_len), :] = s
                m_ref[...] = jnp.maximum(m_ref[...], jnp.max(s.reshape(kb_len // 8, 8, lanes), axis=0))

            @pl.when(jnp.logical_not(need))
            def _():
                s = mm(k_ref[pl.ds(off, kb_len), :], q2, NT)
                s_buf[pl.ds(off, kb_len), :] = s
                m_ref[...] = jnp.maximum(m_ref[...], jnp.max(s.reshape(kb_len // 8, 8, lanes), axis=0))
            return c

        lax.fori_loop(lo, hi, pass1, 0)
        mc = jnp.max(m_ref[...], axis=0, keepdims=True) * cexp
        acc[...] = jnp.zeros_like(acc)

        def pass2(kb, c):
            off = pl.multiple_of(kb * kb_len, kb_len)
            e = jnp.exp2(s_buf[pl.ds(off, kb_len), :] * cexp - mc)
            t = mm(k_ref[pl.ds(off, kb_len), :], t2, NT)
            p = mm(v_ref[pl.ds(off, kb_len), :], g2, NT)
            w1 = e * p
            w2 = e * t
            w3 = w1 * t
            w = jnp.concatenate([e.astype(bf16), w1.astype(bf16), w2.astype(bf16), w3.astype(bf16)], axis=1)
            acc[...] += mm(kt[:, pl.ds(off, kb_len)], w)
            return c

        lax.fori_loop(lo, hi, pass2, 0)
        a = acc[...]
        k0, k1, k2, k3 = (a[0:HS, n * lanes:(n + 1) * lanes] for n in range(4))
        l, aa, bb, cc = (a[HS:HS + 1, n * lanes:(n + 1) * lanes] for n in range(4))
        inv = 1.0 / l
        delta = aa * inv
        mt = bb * inv * scale
        dd = cc * inv * scale - mt * delta
        f = scale * inv
        grad = (k1 - delta * k0) * f
        gdot = (scale * (k3 - delta * k2) - mt * k1 + (mt * delta - dd) * k0) * f
        gh, gl = split2(grad)
        dh, dl = split2(gdot)
        zz = jnp.zeros((16, rows), f32)
        for j in range(tile):
            off = pl.multiple_of((ti * tile + j) * HS, HS)
            bj = b_ref[:, pl.ds(off, HS)]
            tbj = tb_ref[:, pl.ds(off, HS)]
            ln = slice(j * rows, (j + 1) * rows)
            zz += mm(jnp.concatenate([bj, bj, tbj, tbj], 1),
                     jnp.concatenate([dh[:, ln], dl[:, ln], gh[:, ln], gl[:, ln]], 0))
            r = jnp.concatenate([gh[:, ln], gl[:, ln], gh[:, ln], dh[:, ln], dl[:, ln], dh[:, ln]], axis=1)
            bp_ref[:, pl.ds(off, HS)] = mm(llt, r, NT)
        z_ref[...] += zz
        return carry

    lax.fori_loop(0, heads // tile, one_tile, 0)


def attend(docs, seg, low_t, qb, cot, b, tb, k, v, base_fn, kb_len=256):
    rows = qb.shape[0]
    total = k.shape[0]
    sm = pl.BlockSpec(memory_space=pltpu.SMEM)
    vm = pl.BlockSpec(memory_space=pltpu.VMEM)
    return pl.pallas_call(
        functools.partial(attend_kernel, kb_len, base_fn),
        out_shape=(jax.ShapeDtypeStruct((16, rows), f32), jax.ShapeDtypeStruct((16, qb.shape[1]), f32)),
        in_specs=[sm, sm] + [vm] * 8,
        out_specs=(vm, vm),
        scratch_shapes=[
            pltpu.VMEM((total, 2 * rows), f32),
            pltpu.VMEM((HS + 16, total), bf16),
            pltpu.VMEM((HS + 16, 8 * rows), f32),
            pltpu.VMEM((8, 2 * rows), f32),
            pltpu.VMEM((8, rows, HS), bf16),
            pltpu.VMEM((8, rows, HS), bf16),
            pltpu.VMEM((8, rows, HS), bf16),
        ],
        compiler_params=pltpu.CompilerParams(vmem_limit_bytes=40 << 20),
        name="attend",
    )(docs, seg, seg.reshape(1, rows), low_t, qb, cot, b, tb, k, v)


from jax.sharding import PartitionSpec as P

MESH = pl.DeviceIdType.MESH
NX, NC, NZ = 4, 2, 4
GROUP = NX * NC


def place():
    ctx = lax.axis_index("ctx")
    return ctx, ctx // GROUP, (ctx // NC) % NX, ctx % NC


def at(z, x, core):
    return (z % NZ) * GROUP + (x % NX) * NC + core


def greet(ctx_peers, head_peers):
    barrier = pltpu.get_barrier_semaphore()
    for p in ctx_peers:
        pl.semaphore_signal(barrier, inc=1, device_id={"ctx": p}, device_id_type=MESH)
    for p in head_peers:
        pl.semaphore_signal(barrier, inc=1, device_id={"head": p}, device_id_type=MESH)
    return lambda: pl.semaphore_wait(barrier, len(ctx_peers) + len(head_peers))


def gather_kernel(n_head, k_ref, v_ref, x_ref, a_ref, ta_ref, kall, vall, low_ref,
                  parts, mine, rk, rv, rl, ss, sl):
    ctx, z, x, core = place()
    head = lax.axis_index("head")
    rows = k_ref.shape[0]
    heads = [lax.rem(head + d, n_head) for d in range(1, n_head)]
    left, right = at(z, x + 3, core), at(z, x + 1, core)
    down, up = at(z + 3, x, core), at(z + 1, x, core)
    twin = at(z, x, 1 - core)
    ready = greet([left, right, down, up, twin], heads)

    aa = jnp.concatenate([a_ref[...], ta_ref[...]], axis=0)
    part = mm(aa, x_ref[...], NT)
    mine[...] = part
    parts[pl.ds(head, 1)] = part[None]
    own = pl.ds(pl.multiple_of(ctx * rows, rows), rows)
    kall[own, :] = k_ref[...]
    vall[own, :] = v_ref[...]
    ready()

    sends = []

    def cut(ref, j):
        return ref.at[pl.ds(pl.multiple_of(j * rows, rows), rows), :]

    def push(ref, sem, j, to, src=None):
        c = pltpu.make_async_remote_copy(
            src_ref=cut(ref, j) if src is None else src, dst_ref=cut(ref, j), send_sem=ss.at[len(sends)],
            recv_sem=sem.at[j], device_id={"ctx": to}, device_id_type=MESH)
        c.start()
        sends.append(c)

    def push_k(j, to, src=None):
        push(kall, rk, j, to, src)

    def push_v(j, to, src=None):
        push(vall, rv, j, to, src)

    def arrive(ref, sem, j):
        pltpu.make_async_remote_copy(
            src_ref=cut(ref, j), dst_ref=cut(ref, j), send_sem=ss.at[0], recv_sem=sem.at[j],
            device_id={"ctx": twin}, device_id_type=MESH).wait_recv()

    for to in (right, left, up, down, twin):
        push_k(ctx, to, k_ref)
        push_v(ctx, to, v_ref)
    lows = []
    for i, p in enumerate(heads):
        c = pltpu.make_async_remote_copy(
            src_ref=mine, dst_ref=parts.at[head], send_sem=sl.at[i], recv_sem=rl.at[head],
            device_id={"head": p}, device_id_type=MESH)
        c.start()
        lows.append(c)

    def row(zz):
        jl, jr = at(zz, x + 3, core), at(zz, x + 1, core)
        arrive(kall, rk, jl)
        push_k(jl, right)
        arrive(vall, rv, jr)
        push_v(jr, left)
        arrive(vall, rv, jl)
        arrive(kall, rk, jr)
        for j in (jl, jr):
            push_k(j, twin)
            push_v(j, twin)

    def column(j):
        arrive(kall, rk, j)
        for to in (right, left, twin):
            push_k(j, to)
        arrive(vall, rv, j)
        for to in (right, left, twin):
            push_v(j, to)

    jd, ju, jo = at(z + 3, x, core), at(z + 1, x, core), at(z + 2, x, core)
    arrive(kall, rk, jd)
    push_k(jd, up)
    arrive(vall, rv, ju)
    push_v(ju, down)
    for to in (right, left, twin):
        push_k(jd, to)
        push_v(ju, to)
    arrive(vall, rv, jd)
    arrive(kall, rk, ju)
    for to in (right, left, twin):
        push_v(jd, to)
        push_k(ju, to)
    row(z)
    column(jo)
    for i, p in enumerate(heads):
        pltpu.make_async_remote_copy(
            src_ref=mine, dst_ref=parts.at[p], send_sem=sl.at[i], recv_sem=rl.at[p],
            device_id={"head": p}, device_id_type=MESH).wait_recv()
    low_ref[...] = jnp.sum(parts[...], axis=0)
    row(z + 3)
    row(z + 1)
    row(z + 2)
    for d in (0, 3, 1, 2):
        j = at(z + d, x + 2, core)
        arrive(kall, rk, j)
        push_k(j, twin)
        arrive(vall, rv, j)
        push_v(j, twin)
    for zz in range(NZ):
        for xx in range(NX):
            j = at(zz, xx, 1 - core)
            arrive(kall, rk, j)
            arrive(vall, rv, j)
    for c in sends + lows:
        c.wait_send()


def gather(k, v, x, a_t, ta_t, n_ctx, n_head):
    rows, width = k.shape
    vm = pl.BlockSpec(memory_space=pltpu.VMEM)
    return pl.pallas_call(
        functools.partial(gather_kernel, n_head),
        out_shape=(jax.ShapeDtypeStruct((n_ctx * rows, width), bf16), jax.ShapeDtypeStruct((n_ctx * rows, width), bf16),
                   jax.ShapeDtypeStruct((32, rows), f32)),
        in_specs=[vm] * 5,
        out_specs=(vm,) * 3,
        scratch_shapes=[
            pltpu.VMEM((n_head, 32, rows), f32),
            pltpu.VMEM((32, rows), f32),
            pltpu.SemaphoreType.DMA((n_ctx,)),
            pltpu.SemaphoreType.DMA((n_ctx,)),
            pltpu.SemaphoreType.DMA((n_head,)),
            pltpu.SemaphoreType.DMA((64,)),
            pltpu.SemaphoreType.DMA((n_head,)),
        ],
        compiler_params=pltpu.CompilerParams(collective_id=0, has_side_effects=True),
        name="gather",
    )(k, v, x, a_t, ta_t)


def reduce_kernel(n_head, zp_ref, bp_ref, x_ref, oa_ref, ob_ref, zbuf, sa, sb, ra, rb, ca, cb, ta, tb,
                  rz, zs, rsa, rsb, ssa, ssb, rca, rcb, sca, scb, rga, rgb, sga, sgb):
    ctx, z, x, core = place()
    u = lax.rem(ctx, GROUP)
    head = lax.axis_index("head")
    heads = [lax.rem(head + d, n_head) for d in range(1, n_head)]
    mates = [lax.rem(u + d, GROUP) for d in range(1, GROUP)]
    cols = [lax.rem(z + d, NZ) for d in range(1, NZ)]
    ready = greet([z * GROUP + m for m in mates] + [c * GROUP + u for c in cols], heads)
    zbuf[pl.ds(head, 1)] = zp_ref[...][None]
    for i in range(GROUP):
        sb[i] = bp_ref[:, i * HS:(i + 1) * HS]
    ready()
    sends = []

    def copy(src, dst, ssem, rsem, dev):
        return pltpu.make_async_remote_copy(src_ref=src, dst_ref=dst, send_sem=ssem, recv_sem=rsem,
                                            device_id=dev, device_id_type=MESH)

    def start(c):
        c.start()
        sends.append(c)

    for i, p in enumerate(heads):
        start(copy(zp_ref, zbuf.at[head], zs.at[i], rz.at[head], {"head": p}))

    def scatter(s, r, ssem, rsem):
        for i, m in enumerate(mates):
            start(copy(s.at[m], r.at[u], ssem.at[i], rsem.at[u], {"ctx": z * GROUP + m}))
        r[pl.ds(u, 1)] = s[pl.ds(u, 1)]

    def across(r, c, s, rsem, ssem2, rsem2):
        for i, m in enumerate(mates):
            copy(r.at[m], r.at[m], ssem2.at[0], rsem.at[m], {"ctx": z * GROUP + m}).wait_recv()
        part = jnp.sum(r[...], axis=0)
        s[...] = part
        c[pl.ds(z, 1)] = part[None]
        for i, q in enumerate(cols):
            start(copy(s, c.at[z], ssem2.at[i], rsem2.at[z], {"ctx": q * GROUP + u}))

    def spread(c, t, o, ssem, rsem, ssem2, rsem2):
        for i, q in enumerate(cols):
            copy(t.at[q], c.at[q], ssem.at[0], rsem.at[q], {"ctx": q * GROUP + u}).wait_recv()
        t[pl.ds(u, 1)] = jnp.sum(c[...], axis=0)[None]
        for i, m in enumerate(mates):
            start(copy(t.at[u], t.at[u], ssem2.at[i], rsem2.at[u], {"ctx": z * GROUP + m}))

    def collect(t, o, ssem, rsem):
        for m in mates:
            copy(t.at[m], t.at[m], ssem.at[0], rsem.at[m], {"ctx": z * GROUP + m}).wait_recv()
        for i in range(GROUP):
            o[:, i * HS:(i + 1) * HS] = t[i]

    scatter(sb, rb, ssb, rsb)
    for i, p in enumerate(heads):
        copy(zp_ref, zbuf.at[p], zs.at[0], rz.at[p], {"head": p}).wait_recv()
    zsum = jnp.sum(zbuf[...], axis=0)
    ap = mm(jnp.concatenate(split3(zsum), 0), x_ref[...])
    ap = ap[0:16] + ap[16:32] + ap[32:48]
    for i in range(GROUP):
        sa[i] = ap[:, i * HS:(i + 1) * HS]
    scatter(sa, ra, ssa, rsa)
    across(rb, cb, sb_part(sb), rsb, scb, rcb)
    across(ra, ca, sb_part(sa), rsa, sca, rca)
    spread(cb, tb, ob_ref, scb, rcb, sgb, rgb)
    spread(ca, ta, oa_ref, sca, rca, sga, rga)
    collect(tb, ob_ref, sgb, rgb)
    collect(ta, oa_ref, sga, rga)
    for c in sends:
        c.wait_send()


def sb_part(s):
    return s.at[GROUP]


def reduce(zp, bp, x, n_head):
    width = bp.shape[1]
    vm = pl.BlockSpec(memory_space=pltpu.VMEM)
    out = jax.ShapeDtypeStruct((16, width), f32)
    dma = pltpu.SemaphoreType.DMA
    return pl.pallas_call(
        functools.partial(reduce_kernel, n_head),
        out_shape=(out, out),
        in_specs=[vm] * 3,
        out_specs=(vm, vm),
        scratch_shapes=[
            pltpu.VMEM((n_head,) + zp.shape, f32),
            pltpu.VMEM((GROUP + 1, 16, HS), f32), pltpu.VMEM((GROUP + 1, 16, HS), f32),
            pltpu.VMEM((GROUP, 16, HS), f32), pltpu.VMEM((GROUP, 16, HS), f32),
            pltpu.VMEM((NZ, 16, HS), f32), pltpu.VMEM((NZ, 16, HS), f32),
            pltpu.VMEM((GROUP, 16, HS), f32), pltpu.VMEM((GROUP, 16, HS), f32),
            dma((n_head,)), dma((n_head,)),
            dma((GROUP,)), dma((GROUP,)), dma((GROUP,)), dma((GROUP,)),
            dma((NZ,)), dma((NZ,)), dma((NZ,)), dma((NZ,)),
            dma((GROUP,)), dma((GROUP,)), dma((GROUP,)), dma((GROUP,)),
        ],
        compiler_params=pltpu.CompilerParams(collective_id=1, has_side_effects=True),
        name="reduce",
    )(zp, bp, x)


def on_device(n_ctx, n_head, activations, query_base, key_rows, values, out_cotangent, adapter_a, adapter_b, tangent_a, tangent_b,
              segment_ids, doc_starts):
    rows = activations.shape[0]
    kall, vall, low_t = gather(key_rows, values, activations, adapter_a.T, tangent_a.T, n_ctx, n_head)
    zp, bp = attend(doc_starts, segment_ids, low_t, query_base, out_cotangent, adapter_b, tangent_b, kall, vall,
                    base_fn=lambda: lax.axis_index("ctx") * rows, kb_len=KEY_BLOCK)
    oa, ob = reduce(zp, bp, activations, n_head)
    return oa.T, ob


KEY_BLOCK = 1024


def solution(mesh):
    wide = P("ctx", "head")
    placed = (wide,) * 5 + (P("head", None), P(None, "head"), P("head", None), P(None, "head"), P("ctx"), P())
    return jax.shard_map(
        functools.partial(on_device, mesh.shape["ctx"], mesh.shape["head"]),
        mesh=mesh,
        in_specs=placed,
        out_specs=(P("head", None), P(None, "head")),
        check_vma=False,
    )
```

time: 590 us -> 75.2 us (0.13)
  waiting for transfers between devices: 341 us -> 0 us
  matrix products: 119 us -> 0 us
  Pallas kernels: 0 us -> 66 us
  blocking collectives: 43.9 us -> 0 us
  local copies, waits for them, and re-layouts: 46.6 us -> 8.16 us
  other arithmetic: 19.1 us -> 0 us
  between operations: 14.1 us -> 0.73 us
    psum x1 -> x0, waiting for transfers between devices: 264 us -> none  [on_device(): hvp_a, hvp_b = lax.psum((a_part, b_part), 'ctx')]
    dot_general x73 -> x0, matrix products: 119 us -> none  [the longest x16 38.7 us: absorb(): jnp.einsum('trgk,kd->trgd', stacked, key_blk, preferred_element_type=jnp....]
    all_gather x2 -> x0, waiting for transfers between devices: 74.8 us -> none  [the longest x1 52.1 us: on_device(): value_piece = lax.all_gather(values, 'ctx', axis=0, tiled=True)]
    pallas_call x0 -> x3, Pallas kernels: none -> 66 us  [the longest x1 30.1 us: gather(): pl.pallas_call(functools.partial(gather_kernel, n_head), out_shape=(jax.S...]
    psum x2 -> x0, blocking collectives: 43.9 us -> none  [the longest x1 29.1 us: on_device(): adapted = lax.psum(partial_low, 'head')]
    while x608 -> x0, local copies, waits for them, and re-layouts: 27.5 us -> none
    another operation x16 -> x0, other arithmetic: 14.5 us -> none  [absorb(): jnp.stack([weights, weighted_dots, weighted_slopes, weighted_both])]
    exp x16 -> x0, local copies, waits for them, and re-layouts: 11.1 us -> none  [absorb(): factor = jnp.exp(running_max - fresh_max)]
  transfers between devices with their start and end apart: 3 -> 0, of which waited for: 3 -> 0; matrix products, arithmetic and copies ran while one was open for 1% -> 0% of each run, Pallas kernels for 0% -> 0%
where the time goes in v1:
time: 75.2 us; the launch traced here: 74.9 us
  Pallas kernels  66 us (88%)
  local copies, waits for them, and re-layouts  8.16 us (11%)
    pallas_call x1, Pallas kernels, gather(): pl.pallas_call(functools.partial(gather_kernel, n_head), out_shape=(jax.S...  30.1 us
    pallas_call x1, Pallas kernels, reduce(): pl.pallas_call(functools.partial(reduce_kernel, n_head), out_shape=(out,...  29.2 us
    unnamed x26, local copies, waits for them, and re-layouts  8.16 us
    pallas_call x1, Pallas kernels, attend(): pl.pallas_call(functools.partial(attend_kernel, kb_len, base_fn), out_sha...  6.77 us

profile of v1, /device:TPU:1, one launch (start us, length us, event | category | flops | bytes accessed | tf_op | source)
XLA Modules:
  0.0 74.9 jit_solution(10824129991089495127)
XLA Ops:
  0.6 0.0 copy-start.2
  0.6 0.0 copy-start.5
  0.7 0.0 copy-start.6
  0.7 30.1 %gather.1 = (bf16[4096,128]{1,0:T(8,128)(2,1)}, bf16[4096,128]{1,0:T(8,128)(2,1)}, f32[32,128]{1,0:T(8,128)}) custom-call(bf16[128,128]{1,0:T(8,128)(2,1)} %k_ref.1, bf16[128,128]{1,0:T(8,128)(2,1)} %v_ref.1, bf16[128,1024]{1,0:T(8,128)(2,1)} %x_ref.3, bf16[16,1024]{1,0:T(8,128)(2,1)} %bitcast.6, bf16[16,1024]{1,0:T(8,128)(2,1)} %bitcast.7), custom_call_target="tpu_custom_call" | custom-call | tf_op jit(solution)/shard_map/gather/pallas_call | solution.py:309
  30.7 0.0 copy-start.9
  30.8 0.0 copy-start.10
  30.8 0.0 copy-done.2
  30.8 0.0 copy-done.5
  30.8 0.0 copy-done.6
  30.8 0.6 copy-done.9
  31.4 0.0 copy-done.10
  31.4 0.0 copy-start
  31.4 1.2 %copy-done = bf16[4096,128]{1,0:T(8,128)(2,1)S(1)} copy-done((bf16[4096,128]{1,0:T(8,128)(2,1)S(1)}, bf16[4096,128]{1,0:T(8,128)(2,1)}, u32[]{:S(2)}) %copy-start) | copy-done | bytes 1048600
  32.6 0.0 copy-start.1
  32.6 1.2 %copy-done.1 = bf16[4096,128]{1,0:T(8,128)(2,1)S(1)} copy-done((bf16[4096,128]{1,0:T(8,128)(2,1)S(1)}, bf16[4096,128]{1,0:T(8,128)(2,1)}, u32[]{:S(2)}) %copy-start.1) | copy-done | bytes 1048600
  33.9 0.0 copy-start.3
  33.9 0.9 %copy-done.3 = bf16[128,1024]{1,0:T(8,128)(2,1)S(1)} copy-done((bf16[128,1024]{1,0:T(8,128)(2,1)S(1)}, bf16[128,1024]{1,0:T(8,128)(2,1)}, u32[]{:S(2)}) %copy-start.3) | copy-done | bytes 262168
  34.8 0.0 copy-start.7
  34.8 0.7 copy-done.7
  35.5 6.8 %attend.1 = (f32[16,128]{1,0:T(8,128)S(1)}, f32[16,1024]{1,0:T(8,128)S(1)}) custom-call(s32[8]{0:T(128)S(1)} %copy-done.10, s32[128]{0:T(128)S(1)} %copy-done.9, s32[1,128]{1,0:T(1,128)S(1)} %bitcast.4, f32[32,128]{1,0:T(8,128)S(1)} %copy-done.7, bf16[128,1024]{1,0:T(8,128)(2,1)S(1)} %copy-done.2, bf16[128,1024]{1,0:T(8,128)(2,1)S(1)} %copy-done.3, ...), custom_call_target="tpu_custom_call" | custom-call | tf_op jit(solution)/shard_map/attend/pallas_call | solution.py:150
  42.3 0.0 copy-start.4
  42.3 0.7 copy-done.4
  43.0 0.0 copy-start.8
  43.0 0.6 copy-done.8
  43.6 29.2 %reduce.1 = (f32[16,1024]{1,0:T(8,128)}, f32[16,1024]{1,0:T(8,128)}) custom-call(f32[16,128]{1,0:T(8,128)} %copy-done.8, f32[16,1024]{1,0:T(8,128)} %copy-done.4, bf16[128,1024]{1,0:T(8,128)(2,1)} %x_ref.3), custom_call_target="tpu_custom_call" | custom-call | tf_op jit(solution)/shard_map/reduce/pallas_call | solution.py:410
  72.7 0.0 copy-start.11
  72.7 1.5 %copy.15 = f32[1024,16]{0,1:T(8,128)} copy(f32[1024,16]{0,1:T(8,128)} %bitcast.5) | data formatting | bytes 131072
  74.2 0.0 copy-done.11
  74.3 0.6 copy.16
Async XLA Ops:
  0.6 30.1 %copy-start.2 = (bf16[128,1024]{1,0:T(8,128)(2,1)S(1)}, bf16[128,1024]{1,0:T(8,128)(2,1)}, u32[]{:S(2)}) copy-start(bf16[128,1024]{1,0:T(8,128)(2,1)} %qb_ref.1) | copy-start | bytes 786436
  0.6 30.1 %copy-start.5 = (bf16[16,1024]{1,0:T(8,128)(2,1)S(1)}, bf16[16,1024]{1,0:T(8,128)(2,1)}, u32[]{:S(2)}) copy-start(bf16[16,1024]{1,0:T(8,128)(2,1)} %b_ref.1) | copy-start | bytes 98308
  0.7 30.1 %copy-start.6 = (bf16[16,1024]{1,0:T(8,128)(2,1)S(1)}, bf16[16,1024]{1,0:T(8,128)(2,1)}, u32[]{:S(2)}) copy-start(bf16[16,1024]{1,0:T(8,128)(2,1)} %tb_ref.1) | copy-start | bytes 98308
  30.7 0.7 copy-start.9
  30.8 0.7 copy-start.10
  31.4 1.2 %copy-start = (bf16[4096,128]{1,0:T(8,128)(2,1)S(1)}, bf16[4096,128]{1,0:T(8,128)(2,1)}, u32[]{:S(2)}) copy-start(bf16[4096,128]{1,0:T(8,128)(2,1)} %get-tuple-element.10.k_ref) | copy-start | bytes 3145732
  32.6 1.2 %copy-start.1 = (bf16[4096,128]{1,0:T(8,128)(2,1)S(1)}, bf16[4096,128]{1,0:T(8,128)(2,1)}, u32[]{:S(2)}) copy-start(bf16[4096,128]{1,0:T(8,128)(2,1)} %get-tuple-element.11.v_ref) | copy-start | bytes 3145732
  33.9 0.9 %copy-start.3 = (bf16[128,1024]{1,0:T(8,128)(2,1)S(1)}, bf16[128,1024]{1,0:T(8,128)(2,1)}, u32[]{:S(2)}) copy-start(bf16[128,1024]{1,0:T(8,128)(2,1)} %cot_ref.1) | copy-start | bytes 786436
  34.8 0.7 copy-start.7
  42.3 0.7 copy-start.4
  43.0 0.6 copy-start.8
  72.7 1.5 %copy-start.11 = (f32[16,1024]{1,0:T(8,128)S(1)}, f32[16,1024]{1,0:T(8,128)}, u32[]{:S(2)}) copy-start(f32[16,1024]{1,0:T(8,128)} %get-tuple-element.19) | copy-start | bytes 196612

commit v2 on v1

--- a/solution.py
+++ b/solution.py
@@ -192,7 +192,7 @@
 
 
 def gather_kernel(n_head, k_ref, v_ref, x_ref, a_ref, ta_ref, kall, vall, low_ref,
-                  parts, mine, rk, rv, rl, ss, sl):
+                  x_s, a_s, parts, mine, rk, rv, rl, ss, sl, loc):
     ctx, z, x, core = place()
     head = lax.axis_index("head")
     rows = k_ref.shape[0]
@@ -202,41 +202,61 @@
     twin = at(z, x, 1 - core)
     ready = greet([left, right, down, up, twin], heads)
 
-    aa = jnp.concatenate([a_ref[...], ta_ref[...]], axis=0)
-    part = mm(aa, x_ref[...], NT)
-    mine[...] = part
-    parts[pl.ds(head, 1)] = part[None]
-    own = pl.ds(pl.multiple_of(ctx * rows, rows), rows)
-    kall[own, :] = k_ref[...]
-    vall[own, :] = v_ref[...]
-    ready()
-
-    sends = []
-
     def cut(ref, j):
         return ref.at[pl.ds(pl.multiple_of(j * rows, rows), rows), :]
 
-    def push(ref, sem, j, to, src=None):
-        c = pltpu.make_async_remote_copy(
-            src_ref=cut(ref, j) if src is None else src, dst_ref=cut(ref, j), send_sem=ss.at[len(sends)],
-            recv_sem=sem.at[j], device_id={"ctx": to}, device_id_type=MESH)
+    loads = [pltpu.make_async_copy(x_ref, x_s, loc.at[0]), pltpu.make_async_copy(a_ref, a_s.at[0:16], loc.at[1]),
+             pltpu.make_async_copy(ta_ref, a_s.at[16:32], loc.at[2]),
+             pltpu.make_async_copy(k_ref, cut(kall, ctx), loc.at[3]), pltpu.make_async_copy(v_ref, cut(vall, ctx), loc.at[4])]
+    for c in loads:
         c.start()
-        sends.append(c)
-
-    def push_k(j, to, src=None):
-        push(kall, rk, j, to, src)
-
-    def push_v(j, to, src=None):
-        push(vall, rv, j, to, src)
-
-    def arrive(ref, sem, j):
+    ready()
+
+    sends = []
+    count = [0]
+
+    def push(ref, sem, j, tos, cond=None, src=None):
+        for to in tos:
+            n = count[0]
+            count[0] += 1
+
+            def make(n=n, to=to):
+                return pltpu.make_async_remote_copy(
+                    src_ref=cut(ref, j) if src is None else src, dst_ref=cut(ref, j), send_sem=ss.at[n],
+                    recv_sem=sem.at[j], device_id={"ctx": to}, device_id_type=MESH)
+
+            make().start()
+            sends.append((cond, make))
+
+    K, V = (kall, rk), (vall, rv)
+
+    def arrive(kv, j):
+        ref, sem = kv
         pltpu.make_async_remote_copy(
             src_ref=cut(ref, j), dst_ref=cut(ref, j), send_sem=ss.at[0], recv_sem=sem.at[j],
             device_id={"ctx": twin}, device_id_type=MESH).wait_recv()
 
-    for to in (right, left, up, down, twin):
-        push_k(ctx, to, k_ref)
-        push_v(ctx, to, v_ref)
+    def when(cond, f):
+        if cond is None:
+            f()
+        else:
+            pl.when(cond)(f)
+
+    has = {0: None, 1: z >= 1, 2: z >= 2, 3: z >= 3}
+    both, below, first = (z >= 1) & (z <= 2), z <= 2, z == 0
+    spot = [[at(z + NZ - d, x + dx, core) for dx in range(NX)] for d in range(NZ)]
+    other = [[at(z + NZ - d, xx, 1 - core) for xx in range(NX)] for d in range(NZ)]
+    for kv, src in ((K, k_ref), (V, v_ref)):
+        when(below, lambda: push(*kv, ctx, [up], below, src))
+        when(first, lambda: push(*kv, ctx, [down], first, src))
+        push(*kv, ctx, [right, left, twin], None, src)
+
+    loads[0].wait()
+    loads[1].wait()
+    loads[2].wait()
+    part = mm(a_s[...], x_s[...], NT)
+    mine[...] = part
+    parts[pl.ds(head, 1)] = part[None]
     lows = []
     for i, p in enumerate(heads):
         c = pltpu.make_async_remote_copy(
@@ -244,84 +264,95 @@
             device_id={"head": p}, device_id_type=MESH)
         c.start()
         lows.append(c)
-
-    def row(zz):
-        jl, jr = at(zz, x + 3, core), at(zz, x + 1, core)
-        arrive(kall, rk, jl)
-        push_k(jl, right)
-        arrive(vall, rv, jr)
-        push_v(jr, left)
-        arrive(vall, rv, jl)
-        arrive(kall, rk, jr)
-        for j in (jl, jr):
-            push_k(j, twin)
-            push_v(j, twin)
-
-    def column(j):
-        arrive(kall, rk, j)
-        for to in (right, left, twin):
-            push_k(j, to)
-        arrive(vall, rv, j)
-        for to in (right, left, twin):
-            push_v(j, to)
-
-    jd, ju, jo = at(z + 3, x, core), at(z + 1, x, core), at(z + 2, x, core)
-    arrive(kall, rk, jd)
-    push_k(jd, up)
-    arrive(vall, rv, ju)
-    push_v(ju, down)
-    for to in (right, left, twin):
-        push_k(jd, to)
-        push_v(ju, to)
-    arrive(vall, rv, jd)
-    arrive(kall, rk, ju)
-    for to in (right, left, twin):
-        push_v(jd, to)
-        push_k(ju, to)
-    row(z)
-    column(jo)
-    for i, p in enumerate(heads):
-        pltpu.make_async_remote_copy(
-            src_ref=mine, dst_ref=parts.at[p], send_sem=sl.at[i], recv_sem=rl.at[p],
-            device_id={"head": p}, device_id_type=MESH).wait_recv()
-    low_ref[...] = jnp.sum(parts[...], axis=0)
-    row(z + 3)
-    row(z + 1)
-    row(z + 2)
-    for d in (0, 3, 1, 2):
-        j = at(z + d, x + 2, core)
-        arrive(kall, rk, j)
-        push_k(j, twin)
-        arrive(vall, rv, j)
-        push_v(j, twin)
-    for zz in range(NZ):
+    loads[3].wait()
+    loads[4].wait()
+
+    def row(d):
+        jl, jr = spot[d][3], spot[d][1]
+        arrive(K, jl)
+        push(*K, jl, [right, twin], has[d])
+        arrive(K, jr)
+        push(*K, jr, [twin], has[d])
+        arrive(V, jr)
+        push(*V, jr, [left, twin], has[d])
+        arrive(V, jl)
+        push(*V, jl, [twin], has[d])
+
+    def column(d):
+        j = spot[d][0]
+        for kv in (K, V):
+            arrive(kv, j)
+            if d == 1:
+                when(below, lambda: push(*kv, j, [up], both))
+            push(*kv, j, [right, left, twin], has[d])
+
+    def far(d):
+        j = spot[d][2]
+        for kv in (K, V):
+            arrive(kv, j)
+            push(*kv, j, [twin], has[d])
+
+    def low_sum():
+        for i, p in enumerate(heads):
+            pltpu.make_async_remote_copy(
+                src_ref=mine, dst_ref=parts.at[p], send_sem=sl.at[i], recv_sem=rl.at[p],
+                device_id={"head": p}, device_id_type=MESH).wait_recv()
+        low_ref[...] = jnp.sum(parts[...], axis=0)
+
+    row(0)
+    when(has[1], lambda: column(1))
+    when(has[3], lambda: column(3))
+    far(0)
+    low_sum()
+    when(has[1], lambda: row(1))
+    when(has[2], lambda: column(2))
+    when(has[3], lambda: row(3))
+    when(has[1], lambda: far(1))
+    when(has[2], lambda: row(2))
+    when(has[3], lambda: far(3))
+    when(has[2], lambda: far(2))
+
+    def twins(d):
         for xx in range(NX):
-            j = at(zz, xx, 1 - core)
-            arrive(kall, rk, j)
-            arrive(vall, rv, j)
-    for c in sends + lows:
+            j = other[d][xx]
+            arrive(K, j)
+            arrive(V, j)
+
+    for d in range(NZ):
+        when(has[d], lambda: twins(d))
+    groups = {}
+    for cond, make in sends:
+        groups.setdefault(id(cond), (cond, []))[1].append(make)
+
+    def drain(makes):
+        for make in makes:
+            make().wait_send()
+
+    for cond, makes in groups.values():
+        when(cond, lambda: drain(makes))
+    for c in lows:
         c.wait_send()
 
 
 def gather(k, v, x, a_t, ta_t, n_ctx, n_head):
     rows, width = k.shape
     vm = pl.BlockSpec(memory_space=pltpu.VMEM)
+    hb = pl.BlockSpec(memory_space=pltpu.HBM)
+    dma = pltpu.SemaphoreType.DMA
     return pl.pallas_call(
         functools.partial(gather_kernel, n_head),
         out_shape=(jax.ShapeDtypeStruct((n_ctx * rows, width), bf16), jax.ShapeDtypeStruct((n_ctx * rows, width), bf16),
                    jax.ShapeDtypeStruct((32, rows), f32)),
-        in_specs=[vm] * 5,
+        in_specs=[hb] * 5,
         out_specs=(vm,) * 3,
         scratch_shapes=[
+            pltpu.VMEM(x.shape, bf16),
+            pltpu.VMEM((32, x.shape[1]), bf16),
             pltpu.VMEM((n_head, 32, rows), f32),
             pltpu.VMEM((32, rows), f32),
-            pltpu.SemaphoreType.DMA((n_ctx,)),
-            pltpu.SemaphoreType.DMA((n_ctx,)),
-            pltpu.SemaphoreType.DMA((n_head,)),
-            pltpu.SemaphoreType.DMA((64,)),
-            pltpu.SemaphoreType.DMA((n_head,)),
+            dma((n_ctx,)), dma((n_ctx,)), dma((n_head,)), dma((96,)), dma((n_head,)), dma((8,)),
         ],
-        compiler_params=pltpu.CompilerParams(collective_id=0, has_side_effects=True),
+        compiler_params=pltpu.CompilerParams(collective_id=0, has_side_effects=True, vmem_limit_bytes=8 << 20),
         name="gather",
     )(k, v, x, a_t, ta_t)
 
@@ -423,7 +454,7 @@
             dma((NZ,)), dma((NZ,)), dma((NZ,)), dma((NZ,)),
             dma((GROUP,)), dma((GROUP,)), dma((GROUP,)), dma((GROUP,)),
         ],
-        compiler_params=pltpu.CompilerParams(collective_id=1, has_side_effects=True),
+        compiler_params=pltpu.CompilerParams(collective_id=1, has_side_effects=True, vmem_limit_bytes=4 << 20),
         name="reduce",
     )(zp, bp, x)
 

time: 75.2 us -> 71.5 us (0.951)
  Pallas kernels: 66 us -> 63.6 us
  local copies, waits for them, and re-layouts: 8.16 us -> 6.83 us
    pallas_call x1, Pallas kernels: 30.1 us -> 17.6 us  [gather(): pl.pallas_call(functools.partial(gather_kernel, n_head), out_shape=(jax.S...]
    pallas_call x1, Pallas kernels: 29.2 us -> 39.2 us  [reduce(): pl.pallas_call(functools.partial(reduce_kernel, n_head), out_shape=(out,...]
    unnamed x26, local copies, waits for them, and re-layouts: 8.16 us -> 6.83 us
where the time goes in v2:
time: 71.5 us; the launch traced here: 71.1 us
  Pallas kernels  63.6 us (89%)
  local copies, waits for them, and re-layouts  6.83 us (10%)
    pallas_call x1, Pallas kernels, reduce(): pl.pallas_call(functools.partial(reduce_kernel, n_head), out_shape=(out,...  39.2 us
    pallas_call x1, Pallas kernels, gather(): pl.pallas_call(functools.partial(gather_kernel, n_head), out_shape=(jax.S...  17.6 us
    unnamed x26, local copies, waits for them, and re-layouts  6.83 us
    pallas_call x1, Pallas kernels, attend(): pl.pallas_call(functools.partial(attend_kernel, kb_len, base_fn), out_sha...  6.75 us

profile of v2, /device:TPU:1, one launch (start us, length us, event | category | flops | bytes accessed | tf_op | source)
XLA Modules:
  0.0 71.1 jit_solution(11451796909740871089)
XLA Ops:
  0.6 0.0 copy-start
  0.6 0.9 %copy-done = bf16[128,1024]{1,0:T(8,128)(2,1)S(1)} copy-done((bf16[128,1024]{1,0:T(8,128)(2,1)S(1)}, bf16[128,1024]{1,0:T(8,128)(2,1)}, u32[]{:S(2)}) %copy-start) | copy-done | bytes 262168
  1.6 0.0 copy-start.6
  1.6 0.8 %copy-done.6 = bf16[128,128]{1,0:T(8,128)(2,1)S(1)} copy-done((bf16[128,128]{1,0:T(8,128)(2,1)S(1)}, bf16[128,128]{1,0:T(8,128)(2,1)}, u32[]{:S(2)}) %copy-start.6) | copy-done | bytes 32792
  2.3 0.0 copy-start.7
  2.3 0.8 %copy-done.7 = bf16[128,128]{1,0:T(8,128)(2,1)S(1)} copy-done((bf16[128,128]{1,0:T(8,128)(2,1)S(1)}, bf16[128,128]{1,0:T(8,128)(2,1)}, u32[]{:S(2)}) %copy-start.7) | copy-done | bytes 32792
  3.1 0.0 copy-start.8
  3.1 0.8 %copy-done.8 = bf16[1024,16]{0,1:T(8,128)(2,1)S(1)} copy-done((bf16[1024,16]{0,1:T(8,128)(2,1)S(1)}, bf16[1024,16]{0,1:T(8,128)(2,1)}, u32[]{:S(2)}) %copy-start.8) | copy-done | bytes 32792
  3.9 0.0 copy-start.9
  3.9 0.8 %copy-done.9 = bf16[1024,16]{0,1:T(8,128)(2,1)S(1)} copy-done((bf16[1024,16]{0,1:T(8,128)(2,1)S(1)}, bf16[1024,16]{0,1:T(8,128)(2,1)}, u32[]{:S(2)}) %copy-start.9) | copy-done | bytes 32792
  4.6 0.0 copy-start.2
  4.6 0.0 copy-start.4
  4.6 0.0 copy-start.5
  4.6 17.6 %gather.1 = (bf16[4096,128]{1,0:T(8,128)(2,1)S(1)}, bf16[4096,128]{1,0:T(8,128)(2,1)S(1)}, f32[32,128]{1,0:T(8,128)S(1)}) custom-call(bf16[128,128]{1,0:T(8,128)(2,1)S(1)} %copy-done.6, bf16[128,128]{1,0:T(8,128)(2,1)S(1)} %copy-done.7, bf16[128,1024]{1,0:T(8,128)(2,1)S(1)} %copy-done, bf16[16,1024]{1,0:T(8,128)(2,1)S(1)} %bitcast.5, ...), custom_call_target="tpu_custom_call" | custom-call | tf_op jit(solution)/shard_map/gather/pallas_call | solution.py:342
  22.3 0.0 copy-start.10
  22.3 0.0 copy-start.11
  22.3 0.0 copy-done.2
  22.3 0.0 copy-done.4
  22.3 0.0 copy-done.5
  22.3 0.6 copy-done.10
  22.9 0.0 copy-done.11
  22.9 0.0 copy-start.3
  22.9 0.9 %copy-done.3 = bf16[128,1024]{1,0:T(8,128)(2,1)S(1)} copy-done((bf16[128,1024]{1,0:T(8,128)(2,1)S(1)}, bf16[128,1024]{1,0:T(8,128)(2,1)}, u32[]{:S(2)}) %copy-start.3) | copy-done | bytes 262168
  23.9 0.0 copy-start.1
  23.9 6.8 %attend.1 = (f32[16,128]{1,0:T(8,128)S(1)}, f32[16,1024]{1,0:T(8,128)S(1)}) custom-call(s32[8]{0:T(128)S(1)} %copy-done.11, s32[128]{0:T(128)S(1)} %copy-done.10, s32[1,128]{1,0:T(1,128)S(1)} %bitcast.7, f32[32,128]{1,0:T(8,128)S(1)} %get-tuple-element.9.low_ref, bf16[128,1024]{1,0:T(8,128)(2,1)S(1)} %copy-done.2, bf16[128,1024]{1,0:T(8,128)(2,1)S(1)} %copy-done.3, ...), custom_call_target="tpu_custom_call" | custom-call | tf_op jit(solution)/shard_map/attend/pallas_call | solution.py:150
  30.6 0.0 copy-done.1
  30.6 39.2 %reduce.1 = (f32[16,1024]{1,0:T(8,128)S(1)}, f32[16,1024]{1,0:T(8,128)S(1)}) custom-call(f32[16,128]{1,0:T(8,128)S(1)} %get-tuple-element.12.zp_ref, f32[16,1024]{1,0:T(8,128)S(1)} %get-tuple-element.13.bp_ref, bf16[128,1024]{1,0:T(8,128)(2,1)S(1)} %copy-done.1), custom_call_target="tpu_custom_call" | custom-call | tf_op jit(solution)/shard_map/reduce/pallas_call | solution.py:441
  69.9 0.6 copy.15
  70.5 0.6 copy.16
Async XLA Ops:
  0.6 1.0 %copy-start = (bf16[128,1024]{1,0:T(8,128)(2,1)S(1)}, bf16[128,1024]{1,0:T(8,128)(2,1)}, u32[]{:S(2)}) copy-start(bf16[128,1024]{1,0:T(8,128)(2,1)} %x_ref.3) | copy-start | bytes 786436
  1.6 0.8 %copy-start.6 = (bf16[128,128]{1,0:T(8,128)(2,1)S(1)}, bf16[128,128]{1,0:T(8,128)(2,1)}, u32[]{:S(2)}) copy-start(bf16[128,128]{1,0:T(8,128)(2,1)} %k_ref.1) | copy-start | bytes 98308
  2.3 0.8 %copy-start.7 = (bf16[128,128]{1,0:T(8,128)(2,1)S(1)}, bf16[128,128]{1,0:T(8,128)(2,1)}, u32[]{:S(2)}) copy-start(bf16[128,128]{1,0:T(8,128)(2,1)} %v_ref.1) | copy-start | bytes 98308
  3.1 0.8 %copy-start.8 = (bf16[1024,16]{0,1:T(8,128)(2,1)S(1)}, bf16[1024,16]{0,1:T(8,128)(2,1)}, u32[]{:S(2)}) copy-start(bf16[1024,16]{0,1:T(8,128)(2,1)} %param.16) | copy-start | bytes 98308
  3.9 0.8 %copy-start.9 = (bf16[1024,16]{0,1:T(8,128)(2,1)S(1)}, bf16[1024,16]{0,1:T(8,128)(2,1)}, u32[]{:S(2)}) copy-start(bf16[1024,16]{0,1:T(8,128)(2,1)} %param.18) | copy-start | bytes 98308
  4.6 17.7 %copy-start.2 = (bf16[128,1024]{1,0:T(8,128)(2,1)S(1)}, bf16[128,1024]{1,0:T(8,128)(2,1)}, u32[]{:S(2)}) copy-start(bf16[128,1024]{1,0:T(8,128)(2,1)} %qb_ref.1) | copy-start | bytes 786436
  4.6 17.7 %copy-start.4 = (bf16[16,1024]{1,0:T(8,128)(2,1)S(1)}, bf16[16,1024]{1,0:T(8,128)(2,1)}, u32[]{:S(2)}) copy-start(bf16[16,1024]{1,0:T(8,128)(2,1)} %b_ref.1) | copy-start | bytes 98308
  4.6 17.7 %copy-start.5 = (bf16[16,1024]{1,0:T(8,128)(2,1)S(1)}, bf16[16,1024]{1,0:T(8,128)(2,1)}, u32[]{:S(2)}) copy-start(bf16[16,1024]{1,0:T(8,128)(2,1)} %tb_ref.1) | copy-start | bytes 98308
  22.3 0.7 copy-start.10
  22.3 0.7 copy-start.11
  22.9 0.9 %copy-start.3 = (bf16[128,1024]{1,0:T(8,128)(2,1)S(1)}, bf16[128,1024]{1,0:T(8,128)(2,1)}, u32[]{:S(2)}) copy-start(bf16[128,1024]{1,0:T(8,128)(2,1)} %cot_ref.1) | copy-start | bytes 786436
  23.9 6.8 %copy-start.1 = (bf16[128,1024]{1,0:T(8,128)(2,1)S(1)}, bf16[128,1024]{1,0:T(8,128)(2,1)}, u32[]{:S(2)}) copy-start(bf16[128,1024]{1,0:T(8,128)(2,1)} %x_ref.3) | copy-start | bytes 786436
